TPU v7x, 256 devices: a whole 4x4x8 slice. The times are simulated.
256 devices in a mesh: row: 8 (over z), col: 32 (over y, x, core).
Axes of the slice: x: 4, y: 4, z: 8, core: 2. Of those that a mesh axis runs over, the one named last changes fastest.
Arguments:
- amps: bfloat16 [384, 131072], P('row', 'col'), may hold values from -6 to 6
- integrals: bfloat16 [131072, 8192], P('col', 'row'), may hold values from -0.046875 to 0.046875
- cd_first: int32 [131072], P('col'), may hold values from 0 to 2399
- cd_second: int32 [131072], P('col'), may hold values from 0 to 2399
- ab_first: int32 [8192], P('row'), may hold values from 0 to 2399
- ab_second: int32 [8192], P('row'), may hold values from 0 to 2399
- occ_first: int32 [384], P('col'), may hold values from 0 to 199
- occ_second: int32 [384], P('col'), may hold values from 0 to 199
- virt_irrep: int32 [2400], replicated, may hold values from 0 to 7
- occ_energy: float32 [200], replicated, may hold values from -2 to -0.5
- virt_energy: float32 [2400], replicated, may hold values from 0.2 to 3
Outputs:
- update: float32 [384, 8192], P('col', 'row')
All inputs are finite; a program needn't handle non-finite values.
Results may differ from a plain program's by a relative error of at most 0.0003.
Values may be sent and summed in bfloat16 or wider, within the bound.
No kernel may reach another device: no remote copies, remote signals or barrier semaphores. Data moves between devices by JAX's collectives and lax.ppermute only.
A program may use at most 64 MiB of HBM per device.

v0:
```python
import jax
import jax.numpy as jnp
from jax import lax
from jax.sharding import PartitionSpec as P


def table_lookup(values_table, positions):
    row_width = 64
    row_count = -(-values_table.shape[0] // row_width)
    padded_table = jnp.pad(
        values_table, (0, row_count * row_width - values_table.shape[0])
    ).reshape(row_count, row_width)
    high_hot = (
        (positions // row_width)[:, None] == jnp.arange(row_count, dtype=jnp.int32)[None, :]
    ).astype(jnp.float32)
    low_hot = (
        (positions % row_width)[:, None] == jnp.arange(row_width, dtype=jnp.int32)[None, :]
    ).astype(jnp.float32)
    picked = jnp.dot(
        high_hot, padded_table, precision=lax.Precision.HIGHEST, preferred_element_type=jnp.float32
    )
    return jnp.sum(picked * low_hot, axis=1)


def irrep_of(labels_float, first_orb, second_orb):
    first_label = table_lookup(labels_float, first_orb).astype(jnp.int32)
    second_label = table_lookup(labels_float, second_orb).astype(jnp.int32)
    return jnp.bitwise_xor(first_label, second_label)


def on_device(
    amps,
    integrals,
    cd_first,
    cd_second,
    ab_first,
    ab_second,
    occ_first,
    occ_second,
    virt_irrep,
    occ_energy,
    virt_energy,
):
    labels_float = virt_irrep.astype(jnp.float32)
    irrep_cd = irrep_of(labels_float, cd_first, cd_second)
    irrep_ab = irrep_of(labels_float, ab_first, ab_second)
    masked = jnp.where(irrep_cd[:, None] == irrep_ab[None, :], integrals, jnp.zeros_like(integrals))
    partial_sums = jnp.dot(
        lax.all_gather(amps, "row", axis=0, tiled=True), masked, preferred_element_type=jnp.float32
    )
    own_rows = occ_first.shape[0]
    summed = lax.psum(partial_sums, "col")
    ladder = lax.dynamic_slice_in_dim(summed, lax.axis_index("col") * own_rows, own_rows, 0)
    virt_part = table_lookup(virt_energy, ab_first) + table_lookup(virt_energy, ab_second)
    occ_part = table_lookup(occ_energy, occ_first) + table_lookup(occ_energy, occ_second)
    denom = virt_part[None, :] - occ_part[:, None]
    return ladder / denom


def solution(mesh):
    in_specs = (
        P("row", "col"),
        P("col", "row"),
        P("col"),
        P("col"),
        P("row"),
        P("row"),
        P("col"),
        P("col"),
        P(),
        P(),
        P(),
    )
    out_specs = P("col", "row")
    return jax.shard_map(
        on_device, mesh=mesh, in_specs=in_specs, out_specs=out_specs, check_vma=False
    )
```

profile of v0, /device:TPU:6, one launch (start us, length us, event | category | flops | bytes accessed | tf_op | source)
XLA Modules:
  0.0 190.4 jit_solution(7204045527473177920)
XLA Ops:
  6.5 0.7 all-gather.2.cloned.1.call-update
  7.3 0.0 all-reduce.5.cloned.1.call-start
  7.3 0.7 convert_element_type.57
  8.0 0.1 reshape.50
  8.1 0.7 add_select_fusion.5
  8.8 0.6 fusion.8
  9.4 0.7 add_select_fusion.7
  10.1 0.6 fusion.7
  10.7 0.7 add_select_fusion.2
  11.4 0.7 fusion.5
  12.1 0.7 add_select_fusion
  12.8 0.7 fusion.6
  13.6 0.0 copy-start.1
  13.6 43.5 %all-gather.2.cloned.1.call-done = bf16[384,4096]{1,0:T(8,128)(2,1)} async-done(((bf16[48,4096]{1,0:T(8,128)(2,1)}), bf16[384,4096]{1,0:T(8,128)(2,1)}) %all-gather.2.cloned.1.call-update) | async-done | bytes 3145744 | tf_op jit(solution)/shard_map/all_gather | solution.py:49
  57.1 9.0 %fusion.4 = f32[384,1024]{1,0:T(8,128)} fusion(bf16[384,4096]{1,0:T(8,128)(2,1)} %all-gather.2.cloned.1.call-done, bf16[4096,1024]{1,0:T(8,128)(2,1)} %param.12, s32[1024]{0:T(1024)S(1)} %convert_xor_fusion.1, s32[4096]{0:T(1024)S(1)} %convert_xor_fusion), kind=kOutput, calls=%fused_computation.7 | convolution fusion | flops 3229614080 | bytes 13127680 | tf_op jit(solution)/shard_map/dot_general | solution.py:48
  66.1 0.0 all-reduce.5.cloned.1.call-update
  66.2 0.1 reshape.52
  66.2 0.1 reshape.51
  66.3 0.3 fusion.11
  66.6 0.3 fusion.12
  67.0 0.6 fusion.10
  67.5 0.6 fusion.9
  68.1 113.8 %all-reduce.5.cloned.1.call-done = f32[384,1024]{1,0:T(8,128)} async-done(((f32[384,1024]{1,0:T(8,128)}), f32[384,1024]{1,0:T(8,128)}) %all-reduce.5.cloned.1.call-update) | async-done | bytes 1572880 | tf_op jit(solution)/shard_map/psum | solution.py:52
  181.9 1.6 subtract_divide_fusion
  (17 shorter events, 0.1 us)
Async XLA Ops:
  6.5 50.5 %all-gather.2.cloned.1.call-start = ((), (), s32[]{:S(2)}) async-start(), calls=%async_computation | async-start | bytes 3538944 | tf_op jit(solution)/shard_map/all_gather | solution.py:49
  7.3 174.7 %all-reduce.5.cloned.1.call-start = ((), (), s32[]{:S(2)}) async-start(), calls=%async_computation.1 | async-start | bytes 3145728 | tf_op jit(solution)/shard_map/psum | solution.py:52
  13.5 52.5 %copy-start.2 = (s32[12]{0:T(128)S(1)}, s32[12]{0:T(128)}, u32[]{:S(2)}) copy-start(s32[12]{0:T(128)} %param.17) | copy-start | bytes 148
  13.6 52.6 %copy-start.1 = (f32[200]{0:T(256)S(1)}, f32[200]{0:T(256)}, u32[]{:S(2)}) copy-start(f32[200]{0:T(256)} %param.20) | copy-start | bytes 2404
  13.6 52.7 %copy-start = (f32[2400]{0:T(1024)S(1)}, f32[2400]{0:T(1024)}, u32[]{:S(2)}) copy-start(f32[2400]{0:T(1024)} %param.21) | copy-start | bytes 28804
  13.6 53.0 %copy-start.3 = (s32[12]{0:T(128)S(1)}, s32[12]{0:T(128)}, u32[]{:S(2)}) copy-start(s32[12]{0:T(128)} %param.18) | copy-start | bytes 148
Sparse Core Ops, SparseCore 0:
  9.1 47.8 all-gather.1
  66.2 115.6 all-reduce.4
where the time goes:
time: 191 us; the launch traced here: 190 us
  waiting for transfers between devices  158 us (83%)
  between operations  13.5 us (7%)
  matrix products  13.3 us (7%)
  other arithmetic  5.24 us (3%)
    psum x1, waiting for transfers between devices, on_device(): summed = lax.psum(partial_sums, 'col')  114 us
    all_gather x1, waiting for transfers between devices, on_device(): lax.all_gather(amps, 'row', axis=0, tiled=True)  43.5 us
    dot_general x1, matrix products, on_device(): jnp.dot(lax.all_gather(amps, 'row', axis=0, tiled=True), masked, preferre...  9 us
    dot_general x8, matrix products, table_lookup(): jnp.dot(high_hot, padded_table, precision=lax.Precision.HIGHEST, preferre...  4.28 us
  transfers between devices with their start and end apart: 2, of which 2 were waited for; matrix products, arithmetic and copies ran while one was open for 4% of the time, Pallas kernels for 0%

commit v1 on v0

--- a/solution.py
+++ b/solution.py
@@ -2,6 +2,7 @@
 import jax.numpy as jnp
 from jax import lax
 from jax.sharding import PartitionSpec as P
+from jax.lax import axis_size, ppermute
 
 
 def table_lookup(values_table, positions):
@@ -41,6 +42,22 @@
     occ_energy,
     virt_energy,
 ):
+
+    def _read_copies(raw):
+        n_blocks = axis_size("col")
+
+        def _tell_rows(carry_in, latest):
+            if latest >= n_blocks:
+                return carry_in
+            cards = []
+            for s in range(n_blocks):
+                cards.append((s, s ^ latest))
+            return _tell_rows(
+                carry_in + ppermute(carry_in, axis_name="col", perm=cards), 2 * latest
+            )
+
+        return _tell_rows(raw, 1)
+
     labels_float = virt_irrep.astype(jnp.float32)
     irrep_cd = irrep_of(labels_float, cd_first, cd_second)
     irrep_ab = irrep_of(labels_float, ab_first, ab_second)
@@ -49,7 +66,7 @@
         lax.all_gather(amps, "row", axis=0, tiled=True), masked, preferred_element_type=jnp.float32
     )
     own_rows = occ_first.shape[0]
-    summed = lax.psum(partial_sums, "col")
+    summed = _read_copies(partial_sums)
     ladder = lax.dynamic_slice_in_dim(summed, lax.axis_index("col") * own_rows, own_rows, 0)
     virt_part = table_lookup(virt_energy, ab_first) + table_lookup(virt_energy, ab_second)
     occ_part = table_lookup(occ_energy, occ_first) + table_lookup(occ_energy, occ_second)

time: 191 us -> 222 us (1.16)
  waiting for transfers between devices: 158 us -> 183 us
  starting transfers between devices: 0.04 us -> 7.27 us
    ppermute x0 -> x5, waiting for transfers between devices: none -> 138 us  [_tell_rows(): ppermute(carry_in, axis_name='col', perm=cards)]
    psum x1 -> x0, waiting for transfers between devices: 114 us -> none  [on_device(): summed = lax.psum(partial_sums, 'col')]
    ppermute x0 -> x5, starting transfers between devices: none -> 7.27 us  [_tell_rows(): ppermute(carry_in, axis_name='col', perm=cards)]
  transfers between devices with their start and end apart: 2 -> 6, of which waited for: 2 -> 6; matrix products, arithmetic and copies ran while one was open for 4% -> 4% of each run, Pallas kernels for 0% -> 0%
where the time goes in v1:
time: 222 us; the launch traced here: 221 us
  waiting for transfers between devices  183 us (82%)
  between operations  13.5 us (6%)
  matrix products  12.1 us (5%)
  starting transfers between devices  7.27 us (3%)
  other arithmetic  5.55 us (2%)
    ppermute x5, waiting for transfers between devices, _tell_rows(): ppermute(carry_in, axis_name='col', perm=cards)  138 us
    all_gather x1, waiting for transfers between devices, on_device(): lax.all_gather(amps, 'row', axis=0, tiled=True)  43.6 us
    dot_general x1, matrix products, on_device(): jnp.dot(lax.all_gather(amps, 'row', axis=0, tiled=True), masked, preferre...  7.85 us
    ppermute x5, starting transfers between devices, _tell_rows(): ppermute(carry_in, axis_name='col', perm=cards)  7.27 us
  transfers between devices with their start and end apart: 6, of which 6 were waited for; matrix products, arithmetic and copies ran while one was open for 4% of the time, Pallas kernels for 0%

profile of v1, /device:TPU:6, one launch (start us, length us, event | category | flops | bytes accessed | tf_op | source)
XLA Modules:
  0.0 221.4 jit_solution(10766949934199210422)
XLA Ops:
  6.5 0.7 all-gather.2.cloned.1.call-update
  7.3 0.7 convert_element_type.57
  8.0 0.7 add_select_fusion.5
  8.7 0.6 fusion.8
  9.3 0.7 add_select_fusion.7
  10.0 0.6 fusion.7
  10.6 0.7 add_select_fusion.2
  11.3 0.7 fusion.5
  12.0 0.7 add_select_fusion
  12.8 0.7 fusion.6
  13.5 43.6 %all-gather.2.cloned.1.call-done = bf16[384,4096]{1,0:T(8,128)(2,1)} async-done(((bf16[48,4096]{1,0:T(8,128)(2,1)}), bf16[384,4096]{1,0:T(8,128)(2,1)}) %all-gather.2.cloned.1.call-update) | async-done | bytes 3145744 | tf_op jit(solution)/shard_map/all_gather | solution.py:66
  57.1 7.9 %fusion.4 = f32[384,1024]{1,0:T(8,128)S(1)} fusion(bf16[384,4096]{1,0:T(8,128)(2,1)} %all-gather.2.cloned.1.call-done, bf16[4096,1024]{1,0:T(8,128)(2,1)} %param.12, s32[1024]{0:T(1024)S(1)} %convert_xor_fusion.1, s32[4096]{0:T(1024)S(1)} %convert_xor_fusion), kind=kOutput, calls=%fused_computation.7 | convolution fusion | flops 3229614080 | bytes 13127680 | tf_op jit(solution)/shard_map/dot_general | solution.py:65
  65.0 3.4 %collective-permute-done = f32[384,1024]{1,0:T(8,128)S(1)} collective-permute-done((f32[384,1024]{1,0:T(8,128)S(1)}, f32[384,1024]{1,0:T(8,128)S(1)}, u32[]{:S(2)}, u32[]{:S(2)}) %collective-permute-start) | collective-permute-done | bytes 1572896 | tf_op jit(solution)/shard_map/ppermute | solution.py:56
  68.7 0.9 collective-permute-start.1
  69.6 35.6 %collective-permute-done.1 = f32[384,1024]{1,0:T(8,128)S(1)} collective-permute-done((f32[384,1024]{1,0:T(8,128)S(1)}, f32[384,1024]{1,0:T(8,128)S(1)}, u32[]{:S(2)}, u32[]{:S(2)}) %collective-permute-start.1) | collective-permute-done | bytes 1572896 | tf_op jit(solution)/shard_map/ppermute | solution.py:56
  105.6 1.5 collective-permute-start.2
  107.1 35.7 %collective-permute-done.2 = f32[384,1024]{1,0:T(8,128)S(1)} collective-permute-done((f32[384,1024]{1,0:T(8,128)S(1)}, f32[384,1024]{1,0:T(8,128)S(1)}, u32[]{:S(2)}, u32[]{:S(2)}) %collective-permute-start.2) | collective-permute-done | bytes 1572896 | tf_op jit(solution)/shard_map/ppermute | solution.py:56
  143.2 1.6 collective-permute-start.3
  144.8 33.2 %collective-permute-done.3 = f32[384,1024]{1,0:T(8,128)S(1)} collective-permute-done((f32[384,1024]{1,0:T(8,128)S(1)}, f32[384,1024]{1,0:T(8,128)S(1)}, u32[]{:S(2)}, u32[]{:S(2)}) %collective-permute-start.3) | collective-permute-done | bytes 1572896 | tf_op jit(solution)/shard_map/ppermute | solution.py:56
  178.2 3.1 %collective-permute-start.4 = (f32[384,1024]{1,0:T(8,128)S(1)}, f32[384,1024]{1,0:T(8,128)S(1)}, u32[]{:S(2)}, u32[]{:S(2)}) collective-permute-start(f32[384,1024]{1,0:T(8,128)S(1)} %add.85), channel_id=1, source_target_pairs={{0,16},{1,17},{2,18},{3,19},{4,20},{5,21},{6,22},{7,23},{8,24},{9,... | collective-permute-start | bytes 4718600 | tf_op jit(solution)/shard_map/ppermute | solution.py:56
  182.1 0.6 fusion.10
  182.7 0.6 fusion.9
  183.3 30.5 %collective-permute-done.4 = f32[384,1024]{1,0:T(8,128)S(1)} collective-permute-done((f32[384,1024]{1,0:T(8,128)S(1)}, f32[384,1024]{1,0:T(8,128)S(1)}, u32[]{:S(2)}, u32[]{:S(2)}) %collective-permute-start.4) | collective-permute-done | bytes 1572896 | tf_op jit(solution)/shard_map/ppermute | solution.py:56
  213.9 0.7 fusion.19
  (27 shorter events, 2.2 us)
Async XLA Ops:
  6.5 50.5 %all-gather.2.cloned.1.call-start = ((), (), s32[]{:S(2)}) async-start(), calls=%async_computation | async-start | bytes 3538944 | tf_op jit(solution)/shard_map/all_gather | solution.py:66
  64.9 3.5 %collective-permute-start = (f32[384,1024]{1,0:T(8,128)S(1)}, f32[384,1024]{1,0:T(8,128)S(1)}, u32[]{:S(2)}, u32[]{:S(2)}) collective-permute-start(f32[384,1024]{1,0:T(8,128)S(1)} %fusion.4), channel_id=1, source_target_pairs={{0,1},{1,0},{2,3},{3,2},{4,5},{5,4},{6,7},{7,6},{8,9},{9,8},{10,11... | collective-permute-start | bytes 4718600 | tf_op jit(solution)/shard_map/ppermute | solution.py:56
  68.7 36.5 %collective-permute-start.1 = (f32[384,1024]{1,0:T(8,128)S(1)}, f32[384,1024]{1,0:T(8,128)S(1)}, u32[]{:S(2)}, u32[]{:S(2)}) collective-permute-start(f32[384,1024]{1,0:T(8,128)S(1)} %add.82), channel_id=1, source_target_pairs={{0,2},{1,3},{2,0},{3,1},{4,6},{5,7},{6,4},{7,5},{8,10},{9,11},{10,... | collective-permute-start | bytes 4718600 | tf_op jit(solution)/shard_map/ppermute | solution.py:56
  105.6 37.2 %collective-permute-start.2 = (f32[384,1024]{1,0:T(8,128)S(1)}, f32[384,1024]{1,0:T(8,128)S(1)}, u32[]{:S(2)}, u32[]{:S(2)}) collective-permute-start(f32[384,1024]{1,0:T(8,128)S(1)} %add.83), channel_id=1, source_target_pairs={{0,4},{1,5},{2,6},{3,7},{4,0},{5,1},{6,2},{7,3},{8,12},{9,13},{10,... | collective-permute-start | bytes 4718600 | tf_op jit(solution)/shard_map/ppermute | solution.py:56
  143.1 38.2 %copy-start.1 = (f32[200]{0:T(256)S(1)}, f32[200]{0:T(256)}, u32[]{:S(2)}) copy-start(f32[200]{0:T(256)} %param.20) | copy-start | bytes 2404
  143.1 38.3 %copy-start = (f32[2400]{0:T(1024)S(1)}, f32[2400]{0:T(1024)}, u32[]{:S(2)}) copy-start(f32[2400]{0:T(1024)} %param.21) | copy-start | bytes 28804
  143.2 38.3 %copy-start.2 = (s32[12]{0:T(128)S(1)}, s32[12]{0:T(128)}, u32[]{:S(2)}) copy-start(s32[12]{0:T(128)} %param.18) | copy-start | bytes 148
  143.2 38.3 %copy-start.3 = (s32[12]{0:T(128)S(1)}, s32[12]{0:T(128)}, u32[]{:S(2)}) copy-start(s32[12]{0:T(128)} %param.17) | copy-start | bytes 148
  143.2 34.8 %collective-permute-start.3 = (f32[384,1024]{1,0:T(8,128)S(1)}, f32[384,1024]{1,0:T(8,128)S(1)}, u32[]{:S(2)}, u32[]{:S(2)}) collective-permute-start(f32[384,1024]{1,0:T(8,128)S(1)} %add.84), channel_id=1, source_target_pairs={{0,8},{1,9},{2,10},{3,11},{4,12},{5,13},{6,14},{7,15},{8,0},{9,1},... | collective-permute-start | bytes 4718600 | tf_op jit(solution)/shard_map/ppermute | solution.py:56
  178.2 35.6 %collective-permute-start.4 = (f32[384,1024]{1,0:T(8,128)S(1)}, f32[384,1024]{1,0:T(8,128)S(1)}, u32[]{:S(2)}, u32[]{:S(2)}) collective-permute-start(f32[384,1024]{1,0:T(8,128)S(1)} %add.85), channel_id=1, source_target_pairs={{0,16},{1,17},{2,18},{3,19},{4,20},{5,21},{6,22},{7,23},{8,24},{9,... | collective-permute-start | bytes 4718600 | tf_op jit(solution)/shard_map/ppermute | solution.py:56
Sparse Core Ops, SparseCore 0:
  9.1 47.8 all-gather.1
